TPU v7x, 256 devices: a whole 4x4x8 slice. The times are simulated.
256 devices in a mesh: dp: 8 (over z_hi, x), expert: 32 (over y, z_lo, core).
Axes of the slice: x: 4, y: 4, z: 8 (z_hi: 2, z_lo: 4; z = z_hi * 4 + z_lo), core: 2. Of those that a mesh axis runs over, the one named last changes fastest.
Arguments:
- tokens: bfloat16 [4096, 3584], P('expert'), may hold values from -6 to 6
- expert_ids: int32 [4096, 8], P('expert'), may hold values from 0 to 31, all different within a row; in each aligned block of 128 rows (0 to 127, 128 to 255, ...) at most 48 rows name the same one
- route_weight: float32 [4096, 8], P('expert'), may hold values from 0.1 to 1
- pair_swap: int32 [16], replicated, may hold values from 0 to 1, as said below
- expert_gate: bfloat16 [32, 3584, 2048], P('expert', None, 'dp'), may hold values from -0.09375 to 0.09375
- expert_up: bfloat16 [32, 3584, 2048], P('expert', None, 'dp'), may hold values from -0.09375 to 0.09375
- expert_down: bfloat16 [32, 2048, 3584], P('expert', 'dp'), may hold values from -0.1875 to 0.1875
- shared_gate: bfloat16 [3584, 2048], P(None, 'dp'), may hold values from -0.09375 to 0.09375
- shared_up: bfloat16 [3584, 2048], P(None, 'dp'), may hold values from -0.09375 to 0.09375
- shared_down: bfloat16 [2048, 3584], P('dp'), may hold values from -0.1875 to 0.1875
Outputs:
- layer_out: bfloat16 [4096, 3584], P('expert', 'dp')
Inputs may be any that keep to these rules, and one draw needn't show every extreme that they name: `expert_ids`: each row names 8 different experts; within the rows of one device (aligned blocks of 128 rows) no expert is named more than 48 times, a bound that some block reaches. `pair_swap`: entry 0 is always 1; the other entries are 0 or 1.
All inputs are finite; a program needn't handle non-finite values.
Results may differ from a plain program's by a relative error of at most 0.012.
Values may be sent and summed in bfloat16 or wider, within the bound.
A program may use at most 192 MiB of HBM per device.

v0:
```python
import jax
import jax.numpy as jnp
from jax import lax
from jax.sharding import PartitionSpec as P

routed_scale = 2.5


def local(
    tokens,
    expert_ids,
    route_weight,
    pair_swap,
    expert_gate,
    expert_up,
    expert_down,
    shared_gate,
    shared_up,
    shared_down,
):
    f32 = jnp.float32
    rows = tokens.shape[0]
    experts = lax.axis_size("expert")
    half = experts // 2
    columns = jnp.arange(experts, dtype=jnp.int32)
    swap = jnp.concatenate([pair_swap, pair_swap])
    stored = jnp.where(swap == 1, (columns + half) % experts, columns)
    mix = route_weight / jnp.sum(route_weight, axis=1, keepdims=True)
    dense = jnp.sum(
        jnp.where(
            expert_ids[:, :, None] == stored[None, None, :], routed_scale * mix[:, :, None], 0.0
        ),
        axis=1,
    )
    every = lax.all_gather(tokens, "expert", axis=0, tiled=True)
    mine = lax.all_to_all(dense, "expert", split_axis=1, concat_axis=0, tiled=True)
    gate_val = jnp.dot(every, expert_gate[0], preferred_element_type=f32)
    up_val = jnp.dot(every, expert_up[0], preferred_element_type=f32)
    act = (jax.nn.silu(gate_val) * up_val * mine).astype(jnp.bfloat16)
    part = jnp.dot(act, expert_down[0], preferred_element_type=f32)
    shared_gv = jnp.dot(tokens, shared_gate, preferred_element_type=f32)
    shared_uv = jnp.dot(tokens, shared_up, preferred_element_type=f32)
    shared_act = (jax.nn.silu(shared_gv) * shared_uv).astype(jnp.bfloat16)
    shared_out = jnp.dot(shared_act, shared_down, preferred_element_type=f32)
    first = lax.psum_scatter(part.astype(jnp.bfloat16), "dp", scatter_dimension=1, tiled=True)
    second = lax.psum_scatter(first, "expert", scatter_dimension=0, tiled=True)
    shared_sum = lax.psum_scatter(
        shared_out.astype(jnp.bfloat16), "dp", scatter_dimension=1, tiled=True
    )
    return (second.astype(f32) + shared_sum.astype(f32)).astype(jnp.bfloat16)


def solution(mesh):
    in_specs = (
        P("expert", None),
        P("expert", None),
        P("expert", None),
        P(),
        P("expert", None, "dp"),
        P("expert", None, "dp"),
        P("expert", "dp", None),
        P(None, "dp"),
        P(None, "dp"),
        P("dp", None),
    )
    return jax.shard_map(
        local, mesh=mesh, in_specs=in_specs, out_specs=P("expert", "dp"), check_vma=False
    )
```

profile of v0, /device:TPU:8, one launch (start us, length us, event | category | flops | bytes accessed | tf_op | source)
XLA Modules:
  0.0 980.6 jit_solution(4599210068851855276)
XLA Ops:
  6.5 0.7 all-gather.2.cloned.1.call-update
  7.3 0.7 reduce_sum.18
  8.0 0.8 compare_select_fusion.2
  8.8 0.7 divide_multiply_fusion
  9.5 1.4 select_reduce_fusion
  10.8 9.1 all-to-all-start
  20.0 0.0 reduce-scatter.6.cloned.1.call-start
  20.0 155.0 %all-gather.2.cloned.1.call-done = bf16[4096,3584]{1,0:T(8,128)(2,1)} async-done(((bf16[128,3584]{1,0:T(8,128)(2,1)}), bf16[4096,3584]{1,0:T(8,128)(2,1)}) %all-gather.2.cloned.1.call-update) | async-done | bytes 29360144 | tf_op jit(solution)/shard_map/all_gather | solution.py:35
  175.0 15.2 %fusion.7 = f32[4096,256]{1,0:T(8,128)} fusion(bf16[4096,3584]{1,0:T(8,128)(2,1)} %all-gather.2.cloned.1.call-done, bf16[1,3584,256]{2,1,0:T(8,128)(2,1)} %param.14), kind=kOutput, calls=%fused_computation.9 | convolution fusion | flops 7516192768 | bytes 35389440 | tf_op jit(solution)/shard_map/dot_general | solution.py:37
  190.2 37.4 %convolution_convert_fusion = bf16[4096,3584]{0,1:T(8,128)(2,1)} fusion(bf16[4096,3584]{1,0:T(8,128)(2,1)} %all-gather.2.cloned.1.call-done, f32[4096,256]{1,0:T(8,128)} %fusion.7, f32[4096]{0:T(1024)S(1)} %bitcast.26, bf16[1,256,3584]{2,1,0:T(8,128)(2,1)S(1)} %copy-done, bf16[1,3584,256]{2,1,0:T(8,128)(2,1)} %param.15), kind=kOutput, calls=%fused_computation | convolution fusion | flops 15054405632 | bytes 66600960 | tf_op jit(solution)/shard_map/dot_general | solution.py:40
  227.6 0.0 reduce-scatter.6.cloned.1.call-update
  227.6 0.0 reduce-scatter.10.cloned.1.call-start
  227.6 482.4 %reduce-scatter.6.cloned.1.call-done = bf16[4096,448]{0,1:T(8,128)(2,1)} async-done(((bf16[4096,3584]{0,1:T(8,128)(2,1)}), bf16[4096,448]{0,1:T(8,128)(2,1)}) %reduce-scatter.6.cloned.1.call-update) | async-done | bytes 3670032 | tf_op jit(solution)/shard_map/reduce_scatter | solution.py:45
  710.0 6.4 copy.20
  716.4 0.0 reduce-scatter.10.cloned.1.call-update
  716.4 0.0 reduce-scatter.8.cloned.1.call-start
  716.5 1.1 copy-done.2
  717.6 0.6 copy-done.3
  718.2 0.4 fusion.19
  718.6 4.6 convolution_convert_fusion.1
  723.2 142.2 %reduce-scatter.10.cloned.1.call-done = bf16[128,448]{1,0:T(8,128)(2,1)} async-done(((bf16[4096,448]{1,0:T(8,128)(2,1)}), bf16[128,448]{1,0:T(8,128)(2,1)}) %reduce-scatter.10.cloned.1.call-update) | async-done | bytes 114704
  865.5 1.0 copy.21
  866.5 106.0 %reduce-scatter.8.cloned.1.call-done = bf16[128,448]{0,1:T(8,128)(2,1)} async-done(((bf16[128,3584]{0,1:T(8,128)(2,1)}), bf16[128,448]{0,1:T(8,128)(2,1)}) %reduce-scatter.8.cloned.1.call-update) | async-done | bytes 114704 | tf_op jit(solution)/shard_map/reduce_scatter | solution.py:47
  972.5 1.6 add_convert_fusion
  (9 shorter events, 0.0 us)
Async XLA Ops:
  6.5 183.7 %copy-start = (bf16[1,256,3584]{2,1,0:T(8,128)(2,1)S(1)}, bf16[1,256,3584]{2,1,0:T(8,128)(2,1)}, u32[]{:S(2)}) copy-start(bf16[1,256,3584]{2,1,0:T(8,128)(2,1)} %param.16) | copy-start | bytes 5505028
  6.5 168.5 %all-gather.2.cloned.1.call-start = ((), (), s32[]{:S(2)}) async-start(), calls=%async_computation.4 | async-start | bytes 30277632 | tf_op jit(solution)/shard_map/all_gather | solution.py:35
  10.8 179.3 %all-to-all-start = ((f32[128,32,1]{0,2,1:T(1,128)}), f32[128,32,1]{0,2,1:T(1,128)S(1)}, u32[]{:S(2)}, u32[]{:S(2)}) async-start(f32[128,32,1]{0,2,1:T(1,128)} %bitcast.3), calls=%async_computation | async-start | bytes 32768 | tf_op jit(solution)/shard_map/all_to_all | solution.py:36
  20.0 690.0 %reduce-scatter.6.cloned.1.call-start = ((), (), s32[]{:S(2)}) async-start(), calls=%async_computation.5 | async-start | bytes 33030144 | tf_op jit(solution)/shard_map/reduce_scatter | solution.py:45
  227.6 637.9 %reduce-scatter.10.cloned.1.call-start = ((), (), s32[]{:S(2)}) async-start(), calls=%async_computation.7 | async-start | bytes 4325376
  716.4 1.2 copy-start.2
  716.4 1.8 copy-start.3
  716.4 256.1 %reduce-scatter.8.cloned.1.call-start = ((), (), s32[]{:S(2)}) async-start(), calls=%async_computation.6 | async-start | bytes 1032192 | tf_op jit(solution)/shard_map/reduce_scatter | solution.py:47
  718.6 255.5 %copy-start.1 = (bf16[1,256,3584]{2,1,0:T(8,128)(2,1)S(1)}, bf16[1,256,3584]{2,1,0:T(8,128)(2,1)}, u32[]{:S(2)}) copy-start(bf16[1,256,3584]{2,1,0:T(8,128)(2,1)} %param.16) | copy-start | bytes 5505028
Sparse Core Ops, SparseCore 0:
  9.2 165.7 all-gather.1
  227.7 482.2 reduce-scatter.5
  716.6 148.8 reduce-scatter.9
  869.8 102.6 reduce-scatter.7
where the time goes:
time: 981 us
  waiting for transfers between devices  886 us (90%)
  matrix products  57.5 us (6%)
  between operations  13.2 us (1%)
    reduce_scatter x1, waiting for transfers between devices, local(): lax.psum_scatter(part.astype(jnp.bfloat16), 'dp', scatter_dimension=1, ti...  482 us
    all_gather x1, waiting for transfers between devices, local(): every = lax.all_gather(tokens, 'expert', axis=0, tiled=True)  155 us
    unnamed x5, waiting for transfers between devices  143 us
    reduce_scatter x1, waiting for transfers between devices, local(): lax.psum_scatter(shared_out.astype(jnp.bfloat16), 'dp', scatter_dimension...  106 us
    dot_general x1, matrix products, local(): part = jnp.dot(act, expert_down[0], preferred_element_type=f32)  37.4 us
  transfers between devices with their start and end apart: 5, of which 4 were waited for; matrix products, arithmetic and copies ran while one was open for 3% of the time, Pallas kernels for 0%

commit v1 on v0

--- a/solution.py
+++ b/solution.py
@@ -32,7 +32,9 @@
         ),
         axis=1,
     )
-    every = lax.all_gather(tokens, "expert", axis=0, tiled=True)
+    every = jnp.concatenate(
+        lax.all_to_all(jnp.stack([tokens] * lax.axis_size("expert")), "expert", 0, 0), axis=0
+    )
     mine = lax.all_to_all(dense, "expert", split_axis=1, concat_axis=0, tiled=True)
     gate_val = jnp.dot(every, expert_gate[0], preferred_element_type=f32)
     up_val = jnp.dot(every, expert_up[0], preferred_element_type=f32)

time: 981 us -> 1470 us (1.50)
  waiting for transfers between devices: 886 us -> 1360 us
    all_to_all x0 -> x1, waiting for transfers between devices: none -> 632 us  [local(): lax.all_to_all(jnp.stack([tokens] * lax.axis_size('expert')), 'expert', 0...]
    all_gather x1 -> x0, waiting for transfers between devices: 155 us -> none  [local(): every = lax.all_gather(tokens, 'expert', axis=0, tiled=True)]
    unnamed x5 -> x4, waiting for transfers between devices: 143 us -> 143 us
  transfers between devices with their start and end apart: 5 -> 5, of which waited for: 4 -> 4; matrix products, arithmetic and copies ran while one was open for 3% -> 1% of each run, Pallas kernels for 0% -> 0%
where the time goes in v1:
time: 1470 us
  waiting for transfers between devices  1360 us (93%)
  matrix products  57.6 us (4%)
  local copies, waits for them, and re-layouts  20 us (1%)
  starting transfers between devices  15.3 us (1%)
    all_to_all x1, waiting for transfers between devices, local(): lax.all_to_all(jnp.stack([tokens] * lax.axis_size('expert')), 'expert', 0...  632 us
    reduce_scatter x1, waiting for transfers between devices, local(): lax.psum_scatter(part.astype(jnp.bfloat16), 'dp', scatter_dimension=1, ti...  480 us
    unnamed x4, waiting for transfers between devices  143 us
    reduce_scatter x1, waiting for transfers between devices, local(): lax.psum_scatter(shared_out.astype(jnp.bfloat16), 'dp', scatter_dimension...  105 us
    dot_general x1, matrix products, local(): part = jnp.dot(act, expert_down[0], preferred_element_type=f32)  37.4 us
  transfers between devices with their start and end apart: 5, of which 4 were waited for; matrix products, arithmetic and copies ran while one was open for 1% of the time, Pallas kernels for 0%

profile of v1, /device:TPU:8, one launch (start us, length us, event | category | flops | bytes accessed | tf_op | source)
XLA Modules:
  0.0 1469.0 jit_solution(14508277128556993699)
XLA Ops:
  6.5 10.8 stack.2
  17.4 9.3 all-to-all-start
  26.7 0.1 compare_select_fusion.2
  26.8 0.7 select_reduce_fusion
  27.5 631.9 %all-to-all-done = bf16[32,128,3584]{2,1,0:T(8,128)(2,1)} async-done(((bf16[32,128,3584]{2,1,0:T(8,128)(2,1)}), bf16[32,128,3584]{2,1,0:T(8,128)(2,1)}, u32[]{:S(2)}, u32[]{:S(2)}) %all-to-all-start) | async-done | bytes 29360160 | tf_op jit(solution)/shard_map/all_to_all | solution.py:36
  659.4 5.9 all-to-all-start.1
  665.3 0.0 reduce-scatter.6.cloned.1.call-start
  665.3 15.2 %fusion.7 = f32[4096,256]{1,0:T(8,128)} fusion(bf16[4096,3584]{1,0:T(8,128)(2,1)} %bitcast, bf16[1,3584,256]{2,1,0:T(8,128)(2,1)} %param.14), kind=kOutput, calls=%fused_computation.9 | convolution fusion | flops 7516192768 | bytes 35389440 | tf_op jit(solution)/shard_map/dot_general | solution.py:39
  680.5 37.4 %convolution_convert_fusion = bf16[4096,3584]{0,1:T(8,128)(2,1)} fusion(bf16[4096,3584]{1,0:T(8,128)(2,1)} %bitcast, f32[4096,256]{1,0:T(8,128)} %fusion.7, f32[4096]{0:T(1024)S(1)} %bitcast.27, bf16[1,256,3584]{2,1,0:T(8,128)(2,1)S(1)} %copy-done, bf16[1,3584,256]{2,1,0:T(8,128)(2,1)} %param.15), kind=kOutput, calls=%fused_computation | convolution fusion | flops 15054405632 | bytes 66600960 | tf_op jit(solution)/shard_map/dot_general | solution.py:42
  717.9 0.0 reduce-scatter.6.cloned.1.call-update
  717.9 0.0 reduce-scatter.10.cloned.1.call-start
  718.0 480.3 %reduce-scatter.6.cloned.1.call-done = bf16[4096,448]{0,1:T(8,128)(2,1)} async-done(((bf16[4096,3584]{0,1:T(8,128)(2,1)}), bf16[4096,448]{0,1:T(8,128)(2,1)}) %reduce-scatter.6.cloned.1.call-update) | async-done | bytes 3670032 | tf_op jit(solution)/shard_map/reduce_scatter | solution.py:47
  1198.3 6.4 copy.20
  1204.7 0.0 reduce-scatter.10.cloned.1.call-update
  1204.7 0.0 reduce-scatter.8.cloned.1.call-start
  1204.8 1.1 copy-done.2
  1205.9 0.6 copy-done.3
  1206.5 0.4 fusion.19
  1206.9 4.6 convolution_convert_fusion.1
  1211.5 0.0 reduce-scatter.8.cloned.1.call-update
  1211.5 142.9 %reduce-scatter.10.cloned.1.call-done = bf16[128,448]{1,0:T(8,128)(2,1)} async-done(((bf16[4096,448]{1,0:T(8,128)(2,1)}), bf16[128,448]{1,0:T(8,128)(2,1)}) %reduce-scatter.10.cloned.1.call-update) | async-done | bytes 114704
  1354.4 1.0 copy.21
  1355.4 105.4 %reduce-scatter.8.cloned.1.call-done = bf16[128,448]{0,1:T(8,128)(2,1)} async-done(((bf16[128,3584]{0,1:T(8,128)(2,1)}), bf16[128,448]{0,1:T(8,128)(2,1)}) %reduce-scatter.8.cloned.1.call-update) | async-done | bytes 114704 | tf_op jit(solution)/shard_map/reduce_scatter | solution.py:49
  1460.9 1.6 add_convert_fusion
  (15 shorter events, 0.1 us)
Async XLA Ops:
  6.5 674.0 %copy-start = (bf16[1,256,3584]{2,1,0:T(8,128)(2,1)S(1)}, bf16[1,256,3584]{2,1,0:T(8,128)(2,1)}, u32[]{:S(2)}) copy-start(bf16[1,256,3584]{2,1,0:T(8,128)(2,1)} %param.16) | copy-start | bytes 5505028
  17.3 9.4 copy-start.4
  17.3 9.4 copy-start.6
  17.3 9.5 copy-start.5
  17.4 642.0 %all-to-all-start = ((bf16[32,128,3584]{2,1,0:T(8,128)(2,1)}), bf16[32,128,3584]{2,1,0:T(8,128)(2,1)}, u32[]{:S(2)}, u32[]{:S(2)}) async-start(bf16[32,128,3584]{2,1,0:T(8,128)(2,1)} %stack.2), calls=%async_computation | async-start | bytes 58720256 | tf_op jit(solution)/shard_map/all_to_all | solution.py:36
  659.4 21.1 %all-to-all-start.1 = ((f32[128,32,1]{0,2,1:T(1,128)}), f32[128,32,1]{0,2,1:T(1,128)S(1)}, u32[]{:S(2)}, u32[]{:S(2)}) async-start(f32[128,32,1]{0,2,1:T(1,128)} %bitcast.4), calls=%async_computation.1 | async-start | bytes 32768 | tf_op jit(solution)/shard_map/all_to_all | solution.py:38
  665.3 533.0 %reduce-scatter.6.cloned.1.call-start = ((), (), s32[]{:S(2)}) async-start(), calls=%async_computation.5 | async-start | bytes 33030144 | tf_op jit(solution)/shard_map/reduce_scatter | solution.py:47
  717.9 636.4 %reduce-scatter.10.cloned.1.call-start = ((), (), s32[]{:S(2)}) async-start(), calls=%async_computation.7 | async-start | bytes 4325376
  1204.7 1.2 copy-start.2
  1204.7 1.8 copy-start.3
  1204.7 256.1 %reduce-scatter.8.cloned.1.call-start = ((), (), s32[]{:S(2)}) async-start(), calls=%async_computation.6 | async-start | bytes 1032192 | tf_op jit(solution)/shard_map/reduce_scatter | solution.py:49
  1206.9 255.5 %copy-start.1 = (bf16[1,256,3584]{2,1,0:T(8,128)(2,1)S(1)}, bf16[1,256,3584]{2,1,0:T(8,128)(2,1)}, u32[]{:S(2)}) copy-start(bf16[1,256,3584]{2,1,0:T(8,128)(2,1)} %param.16) | copy-start | bytes 5505028
Sparse Core Ops, SparseCore 0:
  718.1 480.1 reduce-scatter.5
  1204.8 149.4 reduce-scatter.9
  1358.8 101.9 reduce-scatter.7
